TPU v7x, 128 devices: a whole 4x4x4 slice. The times are simulated.
128 devices in a mesh: vel: 8 (over y, z_lo), space: 16 (over x, z_hi, core).
Axes of the slice: x: 4, y: 4, z: 4 (z_hi: 2, z_lo: 2; z = z_hi * 2 + z_lo), core: 2. Of those that a mesh axis runs over, the one named last changes fastest.
Arguments:
- density: float32 [1024, 64, 8, 128], P('vel', 'space'), may hold values from -6 to 6
- limiter: int32 [64, 8, 128], P('space'), may hold values from 0 to 2
- heading: int32 [1024], P('vel'), may hold values from 0 to 1
- courant: float32 [1024], P('vel'), may hold values from 0.1 to 0.9
- kernel_slices: bfloat16 [16, 1024, 1024], P('space', None, 'vel'), may hold values from -0.046875 to 0.046875
Outputs:
- transported: float32 [1024, 64, 8, 128], P('vel', 'space')
- collision: float32 [1024, 64, 8, 128], P('vel', 'space')
Inputs may be any that keep to these rules, and one draw needn't show every extreme that they name: `limiter`: 0 no slope, 1 minmod slope, 2 central slope.
All inputs are finite; a program needn't handle non-finite values.
Results may differ from a plain program's by a relative error of at most 0.0041.
Values may be sent and summed in bfloat16 or wider, within the bound.
No kernel may reach another device: no remote copies, remote signals or barrier semaphores. Data moves between devices by JAX's collectives and lax.ppermute only.
A program may use at most 128 MiB of HBM per device.

v0:
```python
import jax
import jax.numpy as jnp
from jax import lax
from jax.sharding import PartitionSpec as P

V = 1024
SLICES = 16


def extended(shard, sides, width):
    for axis, dim in sides:
        size, length = (lax.axis_size(axis), shard.shape[dim])
        up = [(i, (i + 1) % size) for i in range(size - 1)]
        down = [(j, i) for i, j in up]
        last = lax.slice_in_dim(shard, length - width, length, axis=dim)
        first = lax.slice_in_dim(shard, 0, width, axis=dim)
        before = lax.ppermute(last, axis, up)
        after = lax.ppermute(first, axis, down)
        shard = jnp.concatenate([before, shard, after], axis=dim)
    return shard


def limited_slopes(left_diff, right_diff, limiter):
    minmod_slope = jnp.where(
        left_diff * right_diff > 0,
        jnp.sign(left_diff) * jnp.minimum(jnp.abs(left_diff), jnp.abs(right_diff)),
        jnp.zeros_like(left_diff),
    )
    central = 0.5 * (left_diff + right_diff)
    codes = limiter[None]
    return jnp.where(
        codes == 1, minmod_slope, jnp.where(codes == 2, central, jnp.zeros_like(central))
    )


def make_fold(source, totals, pieces):
    stride = V // SLICES

    def one_slice(counter, running):
        matrix = lax.dynamic_index_in_dim(pieces, counter, 0, keepdims=False)
        projected = lax.dot_general(
            matrix, source, (((0,), (0,)), ((), ())), preferred_element_type=jnp.float32
        )
        weight = lax.dynamic_index_in_dim(source, counter * stride, 0, keepdims=True).astype(
            jnp.float32
        )
        return running + weight * projected

    return lax.fori_loop(0, pieces.shape[0], one_slice, totals)


def local(density, limiter, heading, courant, kernel_slices):
    padded = extended(density, (("space", 1),), 1)
    left_diff = density - padded[:, :-2]
    right_diff = padded[:, 2:] - density
    slopes = limited_slopes(left_diff, right_diff, limiter)
    upwind = (2 * heading - 1).astype(jnp.float32)[:, None, None, None]
    rebuilt = density + 0.5 * upwind * slopes
    rebuilt_pad = extended(rebuilt, (("space", 1),), 1)
    forward = (heading == 1)[:, None, None, None]
    upstream = jnp.where(forward, rebuilt_pad[:, :-2], rebuilt_pad[:, 2:])
    transported = density - courant[:, None, None, None] * (rebuilt - upstream)
    flattened = transported.astype(jnp.bfloat16).reshape(density.shape[0], -1)
    columns = lax.all_to_all(flattened, "vel", split_axis=1, concat_axis=0, tiled=True)
    full_slices = lax.all_gather(kernel_slices, "vel", axis=2, tiled=True)
    initial = jnp.zeros(columns.shape, jnp.float32)
    summed = make_fold(columns, initial, lax.all_gather(full_slices, "space", axis=0, tiled=True))
    restored = lax.all_to_all(summed, "vel", split_axis=0, concat_axis=1, tiled=True)
    return (transported, restored.reshape(density.shape))


def solution(mesh):
    return jax.shard_map(
        local,
        mesh=mesh,
        in_specs=(
            P("vel", "space", None, None),
            P("space", None, None),
            P("vel"),
            P("vel"),
            P("space", None, "vel"),
        ),
        out_specs=(P("vel", "space", None, None), P("vel", "space", None, None)),
        check_vma=False,
    )
```

profile of v0, /device:TPU:1, one launch (start us, length us, event | category | flops | bytes accessed | tf_op | source)
XLA Modules:
  0.0 379.8 jit_solution(10808552207556664224)
XLA Ops:
  7.9 61.5 %all-gather.3.cloned.1.call-done = bf16[1,1024,1024]{2,1,0:T(8,128)(2,1)} async-done(((bf16[1,1024,128]{2,1,0:T(8,128)(2,1)}), bf16[1,1024,1024]{2,1,0:T(8,128)(2,1)}) %all-gather.3.cloned.1.call-update) | async-done | bytes 2097168 | tf_op jit(solution)/shard_map/all_gather | solution.py:65
  71.6 6.6 %collective-permute-start = (f32[128,1,8,128]{0,3,2,1:T(8,128)S(1)}, f32[128,1,8,128]{0,3,2,1:T(8,128)S(1)}, u32[]{:S(2)}, u32[]{:S(2)}) collective-permute-start(f32[128,1,8,128]{0,3,2,1:T(8,128)S(1)} %get-tuple-element.111), channel_id=1, source_target_pairs={{0,1},{1,2},{2,3},{3,4},{4,5},{5,6},{6,7},{7,8},{8,9},{9,10},{10,1... | collective-permute-start | bytes 1572872 | tf_op jit(solution)/shard_map/ppermute | solution.py:17
  80.2 11.6 %collective-permute-done = f32[128,1,8,128]{0,3,2,1:T(8,128)S(1)} collective-permute-done((f32[128,1,8,128]{0,3,2,1:T(8,128)S(1)}, f32[128,1,8,128]{0,3,2,1:T(8,128)S(1)}, u32[]{:S(2)}, u32[]{:S(2)}) %collective-permute-start) | collective-permute-done | bytes 524320 | tf_op jit(solution)/shard_map/ppermute | solution.py:17
  93.8 5.9 %collective-permute-start.2 = (f32[128,1,8,128]{0,3,2,1:T(8,128)S(1)}, f32[128,1,8,128]{0,3,2,1:T(8,128)S(1)}, u32[]{:S(2)}, u32[]{:S(2)}) collective-permute-start(f32[128,1,8,128]{0,3,2,1:T(8,128)S(1)} %get-tuple-element.109), channel_id=1, source_target_pairs={{0,1},{1,2},{2,3},{3,4},{4,5},{5,6},{6,7},{7,8},{8,9},{9,10},{10,1... | collective-permute-start | bytes 1572872 | tf_op jit(solution)/shard_map/ppermute | solution.py:17
  101.6 26.6 %collective-permute-done.2 = f32[128,1,8,128]{0,3,2,1:T(8,128)S(1)} collective-permute-done((f32[128,1,8,128]{0,3,2,1:T(8,128)S(1)}, f32[128,1,8,128]{0,3,2,1:T(8,128)S(1)}, u32[]{:S(2)}, u32[]{:S(2)}) %collective-permute-start.2) | collective-permute-done | bytes 524320 | tf_op jit(solution)/shard_map/ppermute | solution.py:17
  131.4 3.6 all-to-all-start
  135.0 10.2 %all-to-all-done = bf16[128,8,512]{2,0,1:T(8,128)(2,1)S(1)} async-done(((bf16[128,8,512]{2,0,1:T(8,128)(2,1)}), bf16[128,8,512]{2,0,1:T(8,128)(2,1)S(1)}, u32[]{:S(2)}, u32[]{:S(2)}) %all-to-all-start) | async-done | bytes 1048608 | tf_op jit(solution)/shard_map/all_to_all | solution.py:64
  145.2 135.5 %all-gather.5.cloned.1.call-done = bf16[16,1024,1024]{2,1,0:T(8,128)(2,1)} async-done(((bf16[1,1024,1024]{2,1,0:T(8,128)(2,1)}), bf16[16,1024,1024]{2,1,0:T(8,128)(2,1)}) %all-gather.5.cloned.1.call-update) | async-done | bytes 33554448 | tf_op jit(solution)/shard_map/all_gather | solution.py:67
  280.7 51.4 %while.14 = (s32[]{:T(128)}, f32[1024,512]{1,0:T(8,128)S(1)}, bf16[1024,512]{1,0:T(8,128)(2,1)S(1)}, bf16[16,1024,1024]{2,1,0:T(8,128)(2,1)}, s32[]{:T(128)}, /*index=5*/s32[]{:T(128)}, s32[]{:T(128)}, s32[]{:T(128)}) while((s32[]{:T(128)}, f32[1024,512]{1,0:T(8,128)S(1)}, bf16[1024,512]{1,0:T(8,128)(2,1)S(1)}, ...), condition=%wide.region_1.2_spmd.clone, body=%wide.region_0.1_spmd.clone.sunk | while | flops 1075315200 | bytes 7345809 | solution.py:49
  283.9 3.2 select_add_fusion.2
  287.1 3.2 select_add_fusion.2
  290.4 3.2 select_add_fusion.2
  293.6 3.2 select_add_fusion.2
  296.8 3.2 select_add_fusion.2
  300.0 3.2 select_add_fusion.2
  303.2 3.2 select_add_fusion.2
  306.4 3.2 select_add_fusion.2
  309.7 3.2 select_add_fusion.2
  312.9 3.2 select_add_fusion.2
  316.1 3.2 select_add_fusion.2
  319.3 3.2 select_add_fusion.2
  322.5 3.2 select_add_fusion.2
  333.4 4.5 %all-to-all-start.1 = ((f32[8,128,512]{2,1,0:T(8,128)}), f32[8,128,512]{2,1,0:T(8,128)}, u32[]{:S(2)}, u32[]{:S(2)}) async-start(f32[8,128,512]{2,1,0:T(8,128)} %bitcast.23), calls=%async_computation.1 | async-start | bytes 4194304 | tf_op jit(solution)/shard_map/all_to_all | solution.py:68
  339.9 29.2 %all-to-all-done.1 = f32[8,128,512]{2,1,0:T(8,128)} async-done(((f32[8,128,512]{2,1,0:T(8,128)}), f32[8,128,512]{2,1,0:T(8,128)}, u32[]{:S(2)}, u32[]{:S(2)}) %all-to-all-start.1) | async-done | bytes 2097184 | tf_op jit(solution)/shard_map/all_to_all | solution.py:68
  (50 shorter events, 28.7 us)
Async XLA Ops:
  7.2 62.3 %all-gather.3.cloned.1.call-start = ((), (), s32[]{:S(2)}) async-start(), calls=%async_computation.2 | async-start | bytes 2359296 | tf_op jit(solution)/shard_map/all_gather | solution.py:65
  7.9 272.8 %all-gather.5.cloned.1.call-start = ((), (), s32[]{:S(2)}) async-start(), calls=%async_computation.3 | async-start | bytes 35651584 | tf_op jit(solution)/shard_map/all_gather | solution.py:67
  71.5 8.6 %copy-start.4 = (s32[128]{0:T(128)S(1)}, s32[128]{0:T(128)}, u32[]{:S(2)}) copy-start(s32[128]{0:T(128)} %param.9) | copy-start | bytes 1540
  71.5 8.7 %copy-start.2 = (s32[4,8,128]{2,1,0:T(8,128)S(1)}, s32[4,8,128]{2,1,0:T(8,128)}, u32[]{:S(2)}) copy-start(s32[4,8,128]{2,1,0:T(8,128)} %param.8) | copy-start | bytes 49156
  71.6 20.2 %collective-permute-start = (f32[128,1,8,128]{0,3,2,1:T(8,128)S(1)}, f32[128,1,8,128]{0,3,2,1:T(8,128)S(1)}, u32[]{:S(2)}, u32[]{:S(2)}) collective-permute-start(f32[128,1,8,128]{0,3,2,1:T(8,128)S(1)} %get-tuple-element.111), channel_id=1, source_target_pairs={{0,1},{1,2},{2,3},{3,4},{4,5},{5,6},{6,7},{7,8},{8,9},{9,10},{10,1... | collective-permute-start | bytes 1572872 | tf_op jit(solution)/shard_map/ppermute | solution.py:17
  78.2 13.6 %collective-permute-start.1 = (f32[128,1,8,128]{0,3,2,1:T(8,128)S(1)}, f32[128,1,8,128]{0,3,2,1:T(8,128)S(1)}, u32[]{:S(2)}, u32[]{:S(2)}) collective-permute-start(f32[128,1,8,128]{0,3,2,1:T(8,128)S(1)} %get-tuple-element.112), channel_id=1, source_target_pairs={{1,0},{2,1},{3,2},{4,3},{5,4},{6,5},{7,6},{8,7},{9,8},{10,9},{11,1... | collective-permute-start | bytes 1572872 | tf_op jit(solution)/shard_map/ppermute | solution.py:18
  93.7 34.5 %copy-start.3 = (f32[128]{0:T(128)S(1)}, f32[128]{0:T(128)}, u32[]{:S(2)}) copy-start(f32[128]{0:T(128)} %param.10) | copy-start | bytes 1540
  93.8 34.4 %collective-permute-start.2 = (f32[128,1,8,128]{0,3,2,1:T(8,128)S(1)}, f32[128,1,8,128]{0,3,2,1:T(8,128)S(1)}, u32[]{:S(2)}, u32[]{:S(2)}) collective-permute-start(f32[128,1,8,128]{0,3,2,1:T(8,128)S(1)} %get-tuple-element.109), channel_id=1, source_target_pairs={{0,1},{1,2},{2,3},{3,4},{4,5},{5,6},{6,7},{7,8},{8,9},{9,10},{10,1... | collective-permute-start | bytes 1572872 | tf_op jit(solution)/shard_map/ppermute | solution.py:17
  99.7 28.5 %collective-permute-start.3 = (f32[128,1,8,128]{0,3,2,1:T(8,128)S(1)}, f32[128,1,8,128]{0,3,2,1:T(8,128)S(1)}, u32[]{:S(2)}, u32[]{:S(2)}) collective-permute-start(f32[128,1,8,128]{0,3,2,1:T(8,128)S(1)} %get-tuple-element.110), channel_id=1, source_target_pairs={{1,0},{2,1},{3,2},{4,3},{5,4},{6,5},{7,6},{8,7},{9,8},{10,9},{11,1... | collective-permute-start | bytes 1572872 | tf_op jit(solution)/shard_map/ppermute | solution.py:18
  131.4 13.8 %all-to-all-start = ((bf16[128,8,512]{2,0,1:T(8,128)(2,1)}), bf16[128,8,512]{2,0,1:T(8,128)(2,1)S(1)}, u32[]{:S(2)}, u32[]{:S(2)}) async-start(bf16[128,8,512]{2,0,1:T(8,128)(2,1)} %copy.17), calls=%async_computation | async-start | bytes 2097152 | tf_op jit(solution)/shard_map/all_to_all | solution.py:64
  332.1 1.3 copy-start.1
  333.4 4.5 %copy-start = (f32[128,4,8,128]{0,3,2,1:T(8,128)S(1)}, f32[128,4,8,128]{0,3,2,1:T(8,128)}, u32[]{:S(2)}) copy-start(f32[128,4,8,128]{0,3,2,1:T(8,128)} %get-tuple-element.108) | copy-start | bytes 6291460
  333.4 35.7 %all-to-all-start.1 = ((f32[8,128,512]{2,1,0:T(8,128)}), f32[8,128,512]{2,1,0:T(8,128)}, u32[]{:S(2)}, u32[]{:S(2)}) async-start(f32[8,128,512]{2,1,0:T(8,128)} %bitcast.23), calls=%async_computation.1 | async-start | bytes 4194304 | tf_op jit(solution)/shard_map/all_to_all | solution.py:68
Sparse Core Ops, SparseCore 0:
  9.6 59.8 all-gather.2
  71.8 208.8 all-gather.4
where the time goes:
time: 381 us; the launch traced here: 380 us
  waiting for transfers between devices  275 us (72%)
  matrix products  50.7 us (13%)
  starting transfers between devices  24.5 us (6%)
  between operations  14.2 us (4%)
  local copies, waits for them, and re-layouts  10.6 us (3%)
  other arithmetic  3.97 us (1%)
    all_gather x1, waiting for transfers between devices, local(): lax.all_gather(full_slices, 'space', axis=0, tiled=True)  136 us
    all_gather x1, waiting for transfers between devices, local(): full_slices = lax.all_gather(kernel_slices, 'vel', axis=2, tiled=True)  61.5 us
    dot_general x16, matrix products, one_slice(): lax.dot_general(matrix, source, (((0,), (0,)), ((), ())), preferred_eleme...  50.7 us
    ppermute x2, waiting for transfers between devices, extended(): before = lax.ppermute(last, axis, up)  38.2 us
    all_to_all x1, waiting for transfers between devices, local(): lax.all_to_all(summed, 'vel', split_axis=0, concat_axis=1, tiled=True)  29.2 us
    ppermute x2, starting transfers between devices, extended(): before = lax.ppermute(last, axis, up)  12.5 us
    all_to_all x1, waiting for transfers between devices, local(): lax.all_to_all(flattened, 'vel', split_axis=1, concat_axis=0, tiled=True)  10.2 us
  transfers between devices with their start and end apart: 8, of which 6 were waited for; matrix products, arithmetic and copies ran while one was open for 2% of the time, Pallas kernels for 0%

commit v1 on v0

--- a/solution.py
+++ b/solution.py
@@ -62,7 +62,9 @@
     transported = density - courant[:, None, None, None] * (rebuilt - upstream)
     flattened = transported.astype(jnp.bfloat16).reshape(density.shape[0], -1)
     columns = lax.all_to_all(flattened, "vel", split_axis=1, concat_axis=0, tiled=True)
-    full_slices = lax.all_gather(kernel_slices, "vel", axis=2, tiled=True)
+    full_slices = jnp.concatenate(
+        lax.all_to_all(jnp.stack([kernel_slices] * lax.axis_size("vel")), "vel", 0, 0), axis=2
+    )
     initial = jnp.zeros(columns.shape, jnp.float32)
     summed = make_fold(columns, initial, lax.all_gather(full_slices, "space", axis=0, tiled=True))
     restored = lax.all_to_all(summed, "vel", split_axis=0, concat_axis=1, tiled=True)

time: 381 us -> 357 us (0.937)
  waiting for transfers between devices: 275 us -> 215 us
  blocking collectives: 0 us -> 31.9 us
  local copies, waits for them, and re-layouts: 10.6 us -> 18.4 us
    all_gather x1 -> x0, waiting for transfers between devices: 61.5 us -> none  [local(): full_slices = lax.all_gather(kernel_slices, 'vel', axis=2, tiled=True)]
    all_to_all x0 -> x1, blocking collectives: none -> 31.9 us  [local(): lax.all_to_all(jnp.stack([kernel_slices] * lax.axis_size('vel')), 'vel',...]
    ppermute x2, waiting for transfers between devices: 0.01 us -> 5.59 us  [extended(): after = lax.ppermute(first, axis, down)]
    reshape x0 -> x1, local copies, waits for them, and re-layouts: none -> 3.93 us  [local(): jnp.concatenate(lax.all_to_all(jnp.stack([kernel_slices] * lax.axis_size(...]
  transfers between devices with their start and end apart: 8 -> 7, of which waited for: 6 -> 6; matrix products, arithmetic and copies ran while one was open for 2% -> 3% of each run, Pallas kernels for 0% -> 0%
where the time goes in v1:
time: 357 us; the launch traced here: 356 us
  waiting for transfers between devices  215 us (60%)
  matrix products  50.7 us (14%)
  blocking collectives  31.9 us (9%)
  starting transfers between devices  21.3 us (6%)
  local copies, waits for them, and re-layouts  18.4 us (5%)
  between operations  14.2 us (4%)
  other arithmetic  3.97 us (1%)
    all_gather x1, waiting for transfers between devices, local(): lax.all_gather(full_slices, 'space', axis=0, tiled=True)  133 us
    dot_general x16, matrix products, one_slice(): lax.dot_general(matrix, source, (((0,), (0,)), ((), ())), preferred_eleme...  50.7 us
    ppermute x2, waiting for transfers between devices, extended(): before = lax.ppermute(last, axis, up)  36.6 us
    all_to_all x1, blocking collectives, local(): lax.all_to_all(jnp.stack([kernel_slices] * lax.axis_size('vel')), 'vel',...  31.9 us
    all_to_all x1, waiting for transfers between devices, local(): lax.all_to_all(summed, 'vel', split_axis=0, concat_axis=1, tiled=True)  29.2 us
    all_to_all x1, waiting for transfers between devices, local(): lax.all_to_all(flattened, 'vel', split_axis=1, concat_axis=0, tiled=True)  10.1 us
    ppermute x2, starting transfers between devices, extended(): before = lax.ppermute(last, axis, up)  8.88 us
    unnamed x13, local copies, waits for them, and re-layouts  7.28 us
  transfers between devices with their start and end apart: 7, of which 6 were waited for; matrix products, arithmetic and copies ran while one was open for 3% of the time, Pallas kernels for 0%

profile of v1, /device:TPU:1, one launch (start us, length us, event | category | flops | bytes accessed | tf_op | source)
XLA Modules:
  0.0 356.0 jit_solution(5108275356762077209)
XLA Ops:
  8.4 31.9 %all_to_all.40 = bf16[8,1,1024,128]{3,2,1,0:T(8,128)(2,1)S(1)} all-to-all(bf16[8,1,1024,128]{3,2,1,0:T(8,128)(2,1)S(1)} %stack.2), channel_id=1, replica_groups=mesh['vel'=8,'space'=16] {'vel'}, dimensions={0} | all-to-all | bytes 4194304 | tf_op jit(solution)/shard_map/all_to_all | solution.py:66
  42.9 3.9 %copy.19 = bf16[1,1024,1024]{2,1,0:T(8,128)(2,1)} copy(bf16[1,1024,1024]{1,2,0:T(8,128)(2,1)} %bitcast.25) | data formatting | bytes 4194304 | tf_op jit(solution)/shard_map/reshape | solution.py:65
  49.0 7.0 %collective-permute-start = (f32[128,1,8,128]{0,3,2,1:T(8,128)S(1)}, f32[128,1,8,128]{0,3,2,1:T(8,128)S(1)}, u32[]{:S(2)}, u32[]{:S(2)}) collective-permute-start(f32[128,1,8,128]{0,3,2,1:T(8,128)S(1)} %get-tuple-element.111), channel_id=1, source_target_pairs={{0,1},{1,2},{2,3},{3,4},{4,5},{5,6},{6,7},{7,8},{8,9},{9,10},{10,1... | collective-permute-start | bytes 1572872 | tf_op jit(solution)/shard_map/ppermute | solution.py:17
  57.9 10.5 %collective-permute-done = f32[128,1,8,128]{0,3,2,1:T(8,128)S(1)} collective-permute-done((f32[128,1,8,128]{0,3,2,1:T(8,128)S(1)}, f32[128,1,8,128]{0,3,2,1:T(8,128)S(1)}, u32[]{:S(2)}, u32[]{:S(2)}) %collective-permute-start) | collective-permute-done | bytes 524320 | tf_op jit(solution)/shard_map/ppermute | solution.py:17
  68.4 5.6 %collective-permute-done.1 = f32[128,1,8,128]{0,3,2,1:T(8,128)S(1)} collective-permute-done((f32[128,1,8,128]{0,3,2,1:T(8,128)S(1)}, f32[128,1,8,128]{0,3,2,1:T(8,128)S(1)}, u32[]{:S(2)}, u32[]{:S(2)}) %collective-permute-start.1) | collective-permute-done | bytes 524320 | tf_op jit(solution)/shard_map/ppermute | solution.py:18
  80.4 26.1 %collective-permute-done.2 = f32[128,1,8,128]{0,3,2,1:T(8,128)S(1)} collective-permute-done((f32[128,1,8,128]{0,3,2,1:T(8,128)S(1)}, f32[128,1,8,128]{0,3,2,1:T(8,128)S(1)}, u32[]{:S(2)}, u32[]{:S(2)}) %collective-permute-start.2) | collective-permute-done | bytes 524320 | tf_op jit(solution)/shard_map/ppermute | solution.py:17
  109.7 3.6 all-to-all-start
  113.3 10.1 %all-to-all-done = bf16[128,8,512]{2,0,1:T(8,128)(2,1)S(1)} async-done(((bf16[128,8,512]{2,0,1:T(8,128)(2,1)}), bf16[128,8,512]{2,0,1:T(8,128)(2,1)S(1)}, u32[]{:S(2)}, u32[]{:S(2)}) %all-to-all-start) | async-done | bytes 1048608 | tf_op jit(solution)/shard_map/all_to_all | solution.py:64
  123.5 133.4 %all-gather.2.cloned.1.call-done = bf16[16,1024,1024]{2,1,0:T(8,128)(2,1)} async-done(((bf16[1,1024,1024]{2,1,0:T(8,128)(2,1)}), bf16[16,1024,1024]{2,1,0:T(8,128)(2,1)}) %all-gather.2.cloned.1.call-update) | async-done | bytes 33554448 | tf_op jit(solution)/shard_map/all_gather | solution.py:69
  256.9 51.4 %while.14 = (s32[]{:T(128)}, f32[1024,512]{1,0:T(8,128)S(1)}, bf16[1024,512]{1,0:T(8,128)(2,1)S(1)}, bf16[16,1024,1024]{2,1,0:T(8,128)(2,1)}, s32[]{:T(128)}, /*index=5*/s32[]{:T(128)}, s32[]{:T(128)}, s32[]{:T(128)}) while((s32[]{:T(128)}, f32[1024,512]{1,0:T(8,128)S(1)}, bf16[1024,512]{1,0:T(8,128)(2,1)S(1)}, ...), condition=%wide.region_1.2_spmd.clone, body=%wide.region_0.1_spmd.clone.sunk | while | flops 1075315200 | bytes 7345809 | solution.py:49
  260.1 3.2 select_add_fusion.2
  263.3 3.2 select_add_fusion.2
  266.5 3.2 select_add_fusion.2
  269.7 3.2 select_add_fusion.2
  273.0 3.2 select_add_fusion.2
  276.2 3.2 select_add_fusion.2
  279.4 3.2 select_add_fusion.2
  282.6 3.2 select_add_fusion.2
  285.8 3.2 select_add_fusion.2
  289.0 3.2 select_add_fusion.2
  292.3 3.2 select_add_fusion.2
  295.5 3.2 select_add_fusion.2
  309.6 4.5 %all-to-all-start.2 = ((f32[8,128,512]{2,1,0:T(8,128)}), f32[8,128,512]{2,1,0:T(8,128)}, u32[]{:S(2)}, u32[]{:S(2)}) async-start(f32[8,128,512]{2,1,0:T(8,128)} %bitcast.28), calls=%async_computation.2 | async-start | bytes 4194304 | tf_op jit(solution)/shard_map/all_to_all | solution.py:70
  316.1 29.2 %all-to-all-done.2 = f32[8,128,512]{2,1,0:T(8,128)} async-done(((f32[8,128,512]{2,1,0:T(8,128)}), f32[8,128,512]{2,1,0:T(8,128)}, u32[]{:S(2)}, u32[]{:S(2)}) %all-to-all-start.2) | async-done | bytes 2097184 | tf_op jit(solution)/shard_map/all_to_all | solution.py:70
  (51 shorter events, 37.4 us)
Async XLA Ops:
  7.2 249.7 %all-gather.2.cloned.1.call-start = ((), (), s32[]{:S(2)}) async-start(), calls=%async_computation.3 | async-start | bytes 35651584 | tf_op jit(solution)/shard_map/all_gather | solution.py:69
  48.9 9.0 %copy-start.4 = (s32[128]{0:T(128)S(1)}, s32[128]{0:T(128)}, u32[]{:S(2)}) copy-start(s32[128]{0:T(128)} %param.9) | copy-start | bytes 1540
  48.9 9.0 %copy-start.2 = (s32[4,8,128]{2,1,0:T(8,128)S(1)}, s32[4,8,128]{2,1,0:T(8,128)}, u32[]{:S(2)}) copy-start(s32[4,8,128]{2,1,0:T(8,128)} %param.8) | copy-start | bytes 49156
  49.0 19.4 %collective-permute-start = (f32[128,1,8,128]{0,3,2,1:T(8,128)S(1)}, f32[128,1,8,128]{0,3,2,1:T(8,128)S(1)}, u32[]{:S(2)}, u32[]{:S(2)}) collective-permute-start(f32[128,1,8,128]{0,3,2,1:T(8,128)S(1)} %get-tuple-element.111), channel_id=1, source_target_pairs={{0,1},{1,2},{2,3},{3,4},{4,5},{5,6},{6,7},{7,8},{8,9},{9,10},{10,1... | collective-permute-start | bytes 1572872 | tf_op jit(solution)/shard_map/ppermute | solution.py:17
  56.0 18.1 %collective-permute-start.1 = (f32[128,1,8,128]{0,3,2,1:T(8,128)S(1)}, f32[128,1,8,128]{0,3,2,1:T(8,128)S(1)}, u32[]{:S(2)}, u32[]{:S(2)}) collective-permute-start(f32[128,1,8,128]{0,3,2,1:T(8,128)S(1)} %get-tuple-element.112), channel_id=1, source_target_pairs={{1,0},{2,1},{3,2},{4,3},{5,4},{6,5},{7,6},{8,7},{9,8},{10,9},{11,1... | collective-permute-start | bytes 1572872 | tf_op jit(solution)/shard_map/ppermute | solution.py:18
  75.9 30.6 %copy-start.3 = (f32[128]{0:T(128)S(1)}, f32[128]{0:T(128)}, u32[]{:S(2)}) copy-start(f32[128]{0:T(128)} %param.10) | copy-start | bytes 1540
  76.0 30.5 %collective-permute-start.2 = (f32[128,1,8,128]{0,3,2,1:T(8,128)S(1)}, f32[128,1,8,128]{0,3,2,1:T(8,128)S(1)}, u32[]{:S(2)}, u32[]{:S(2)}) collective-permute-start(f32[128,1,8,128]{0,3,2,1:T(8,128)S(1)} %get-tuple-element.109), channel_id=1, source_target_pairs={{0,1},{1,2},{2,3},{3,4},{4,5},{5,6},{6,7},{7,8},{8,9},{9,10},{10,1... | collective-permute-start | bytes 1572872 | tf_op jit(solution)/shard_map/ppermute | solution.py:17
  77.9 28.5 %collective-permute-start.3 = (f32[128,1,8,128]{0,3,2,1:T(8,128)S(1)}, f32[128,1,8,128]{0,3,2,1:T(8,128)S(1)}, u32[]{:S(2)}, u32[]{:S(2)}) collective-permute-start(f32[128,1,8,128]{0,3,2,1:T(8,128)S(1)} %get-tuple-element.110), channel_id=1, source_target_pairs={{1,0},{2,1},{3,2},{4,3},{5,4},{6,5},{7,6},{8,7},{9,8},{10,9},{11,1... | collective-permute-start | bytes 1572872 | tf_op jit(solution)/shard_map/ppermute | solution.py:18
  109.7 13.7 %all-to-all-start = ((bf16[128,8,512]{2,0,1:T(8,128)(2,1)}), bf16[128,8,512]{2,0,1:T(8,128)(2,1)S(1)}, u32[]{:S(2)}, u32[]{:S(2)}) async-start(bf16[128,8,512]{2,0,1:T(8,128)(2,1)} %copy.17), calls=%async_computation | async-start | bytes 2097152 | tf_op jit(solution)/shard_map/all_to_all | solution.py:64
  308.3 1.3 copy-start.1
  309.6 4.5 %copy-start = (f32[128,4,8,128]{0,3,2,1:T(8,128)S(1)}, f32[128,4,8,128]{0,3,2,1:T(8,128)}, u32[]{:S(2)}) copy-start(f32[128,4,8,128]{0,3,2,1:T(8,128)} %get-tuple-element.108) | copy-start | bytes 6291460
  309.6 35.7 %all-to-all-start.2 = ((f32[8,128,512]{2,1,0:T(8,128)}), f32[8,128,512]{2,1,0:T(8,128)}, u32[]{:S(2)}, u32[]{:S(2)}) async-start(f32[8,128,512]{2,1,0:T(8,128)} %bitcast.28), calls=%async_computation.2 | async-start | bytes 4194304 | tf_op jit(solution)/shard_map/all_to_all | solution.py:70
Sparse Core Ops, SparseCore 0:
  47.0 209.8 all-gather.1
